TPU v7x, 32 devices: a whole 2x2x4 slice. The times are simulated.
32 devices in a mesh: groups: 2 (over y), patch: 8 (over z, x), visit: 2 (over core).
Axes of the slice: x: 2, y: 2, z: 4, core: 2. Of those that a mesh axis runs over, the one named last changes fastest.
Arguments:
- visit_tiles: bfloat16 [1792, 64, 1024], P(('groups', 'patch', 'visit')), parts along dimension 0, may hold values from -6 to 6
- tile_patch: int32 [1792], P(('groups', 'patch', 'visit')), parts along dimension 0, may hold values from 0 to 7, as said below
- offsets: int32 [1792, 2], P(('groups', 'patch', 'visit')), parts along dimension 0, may hold values from -128 to 127
- psf_coefs: int32 [1792, 3], P(('groups', 'patch', 'visit')), parts along dimension 0, may hold values from 16 to 80
- weights: bfloat16 [1792], P(('groups', 'patch', 'visit')), parts along dimension 0, may hold values from 0.19921875 to 4
Outputs:
- coadd: float32 [1024, 1024], P(('groups', 'patch')), parts along dimension 0
- detection: float32 [1024, 1024], P(('groups', 'patch')), parts along dimension 0
There are 2 independent parts, one for each index of `groups`. A program takes and returns all parts, laid end to end along the dimension named above; each array names one. Nothing has to cross between parts.
Inputs may be any that keep to these rules, and one draw needn't show every extreme that they name: `tile_patch`: among the 56 tiles of one device at most 14 name any one patch; 2 deep-field patches are named by exactly 14 tiles of every device; every patch is named by some tile.
All inputs are finite; a program needn't handle non-finite values.
Results may differ from a plain program's by a relative error of at most 0.0048.
Values may be sent and summed in bfloat16 or wider, within the bound.
No kernel may reach another device: no remote copies, remote signals or barrier semaphores. Data moves between devices by JAX's collectives and lax.ppermute only.
A program may use at most 128 MiB of HBM per device.

v0:
```python
import functools
import math

import jax
import jax.numpy as jnp
import numpy as np
from jax import lax
from jax.experimental import pallas as pl
from jax.experimental.pallas import tpu as pltpu
from jax.sharding import PartitionSpec as P


BF16, F32, I32 = jnp.bfloat16, jnp.float32, jnp.int32
HALO = 8
PSF_SIGMAS = (0.75, 1.5, 3.0)
PSF_REACH = 16
BASES = len(PSF_SIGMAS)
LANES = 128
WIDE = 2 * LANES
GROUP = 4
PSF_BATCH = 4
STEPS = 64
OFFSET_MAX = 128
WEIGHT_BITS = 10
WARP_SEGMENT, WARP_EDGE = 32, 8
PSF_SEGMENT, PSF_EDGE = 64, 16


def gaussian(distance, sigma, reach):
    shape = np.exp(-distance * distance / (2.0 * sigma * sigma)) / (math.pi * sigma * sigma) ** 0.25
    return np.where(np.abs(distance) <= reach, shape, 0.0)


def to_bf16(value):
    return value.astype(np.float32).astype(BF16)


def row_filters(rows):
    index = np.arange(rows, dtype=np.float64)
    offset = index[:, None] - index[None, :]
    stacked = np.concatenate([gaussian(offset, s, PSF_REACH) for s in PSF_SIGMAS], axis=0)
    high = to_bf16(stacked)
    return np.concatenate([high, to_bf16(stacked - high.astype(np.float64))], axis=1)


def psf_col_filters():
    lane = np.arange(WIDE, dtype=np.float64)
    offset = lane[None, :] - lane[:, None]
    same = (lane[None, :] // PSF_SEGMENT) == (lane[:, None] // PSF_SEGMENT)
    bands = [gaussian(offset, s, PSF_REACH) for s in PSF_SIGMAS]
    main = np.concatenate(bands, axis=0)
    edge = np.concatenate([np.where(same, band, 0.0) for band in bands], axis=0)
    return to_bf16(main), to_bf16(edge)


def col_filter(sigma, reach):
    lane = np.arange(LANES, dtype=np.float64)
    offset = lane[None, :] - lane[:, None]
    wrapped = (offset + LANES // 2) % LANES - LANES // 2
    circulant = gaussian(wrapped, sigma, reach)
    own = np.where(np.abs(offset) < LANES // 2, circulant, 0.0)
    edge = np.where(np.abs(offset) >= LANES // 2, circulant, 0.0)
    return to_bf16(np.concatenate([own, edge], axis=0))


def lanczos_lines():
    lane = np.arange(LANES, dtype=np.float64)
    wrapped = (lane + LANES // 2) % LANES - LANES // 2
    offset = np.arange(-OFFSET_MAX, OFFSET_MAX + 8, dtype=np.float64)[:, None] / STEPS
    value = wrapped[None, :] + offset
    line = np.where(np.abs(value) < 3.0, np.sinc(value) * np.sinc(value / 3.0), 0.0)
    return line.astype(np.float32)


def digit_bits(devices):
    return max(1, int(math.log2(256 // devices)) if devices <= 128 else 1)


def power_of_two(exponent):
    out = 1.0
    for i in range(6):
        out = out * jnp.where((exponent >> i) & 1 == 1, 2.0 ** (2**i), 1.0)
    return out


def windows(blocks):
    rows = blocks[0].shape[0]
    left = lax.broadcasted_iota(I32, (rows, LANES), 1) < LANES // 2
    zero = jnp.zeros_like(blocks[0])
    padded = [zero, *blocks, zero]
    return jnp.concatenate(
        [
            jnp.concatenate([padded[b + 1], jnp.where(left, padded[b + 2], padded[b])], axis=1)
            for b in range(len(blocks))
        ],
        axis=0,
    )


def block(value, b):
    return value[:, b * LANES : (b + 1) * LANES]


def border_columns(value, segment):
    rows, cols = value.shape
    lane = lax.broadcasted_iota(I32, (rows, LANES), 1)
    per = LANES // segment
    borders = cols // WIDE - 1
    out = []
    for start in range(0, borders, per):
        merged = None
        for s in range(start, min(start + per, borders)):
            both = jnp.where(lane < LANES // 2, block(value, 2 * s + 2), block(value, 2 * s + 1))
            moved = pltpu.roll(both, segment // 2 + segment * (s - start), 1)
            merged = moved if merged is None else jnp.where(lane >= segment * (s - start), moved, merged)
        out.append(merged)
    return out


def mend_borders(blocks, edges, segment, reach):
    rows = blocks[0].shape[0]
    lane = lax.broadcasted_iota(I32, (rows, LANES), 1)
    per = LANES // segment
    blocks = list(blocks)
    for s in range(len(blocks) // 2 - 1):
        shift = LANES - segment // 2 - segment * (s % per)
        moved = pltpu.roll(edges[s // per], shift, 1)
        blocks[2 * s + 1] = jnp.where(lane >= LANES - reach, moved, blocks[2 * s + 1])
        blocks[2 * s + 2] = jnp.where(lane < reach, moved, blocks[2 * s + 2])
    return blocks


def side_by_side(value):
    return jnp.concatenate(
        [value[:, s : s + WIDE] for s in range(0, value.shape[1], WIDE)], axis=0
    )


def stack_kernel(
    bits,
    tile_patch_in,
    raw_weights_in,
    offsets_in,
    coefs_in,
    tiles,
    lines_in,
    row_mats_in,
    col_main_in,
    col_edge_in,
    first_send,
    rest_send,
    first_keep,
    rest_keep,
    raw,
    shifted,
    mixers,
    total,
    stacked,
    strip,
    sems,
    tile_patch,
    raw_weights,
    offsets,
    coefs,
    lines,
    row_mats,
    col_main,
    col_edge,
    in_sems,
    weight_line,
    weight_sem,
    weights,
    weight_sq,
    order,
    first,
    cursor,
    rounded,
    out_sems,
):
    me = lax.axis_index("patch")
    helper = lax.axis_index("visit")
    count, rows, cols = tiles.shape
    patches = stacked.shape[0]
    near = (rows + 2 * HALO) // 2

    moves = [
        pltpu.make_async_copy(source, target, in_sems.at[i])
        for i, (source, target) in enumerate(
            (
                (tile_patch_in, tile_patch),
                (raw_weights_in, raw_weights),
                (offsets_in, offsets),
                (coefs_in, coefs),
                (lines_in, lines),
                (row_mats_in, row_mats),
                (col_main_in, col_main),
                (col_edge_in, col_edge),
            )
        )
    ]
    for move in moves:
        move.start()
    for k in range(patches):
        cursor[k] = 0
        weight_sq[k] = 0.0
    moves[0].wait()
    for t in range(count):
        cursor[tile_patch[t]] += 1
    running = 0
    for k in range(patches):
        number = cursor[k]
        first[k] = running
        cursor[k] = running
        running = running + number
    for t in range(count):
        key = tile_patch[t]
        slot = cursor[key]
        cursor[key] = slot + 1
        order[slot] = t

    groups = -(-count // GROUP)

    def tile_at(g, j):
        return order[jnp.minimum(g * GROUP + j, count - 1)]

    def key_at(g, j):
        slot = g * GROUP + j
        key = tile_patch[order[jnp.minimum(slot, count - 1)]]
        return key if count % GROUP == 0 else jnp.where(slot < count, key, -1)

    def fetch(g, carry):
        for j in range(GROUP):
            pltpu.make_async_copy(tiles.at[tile_at(g, j)], raw.at[g, j], sems.at[g]).start()
        return carry

    lax.fori_loop(0, groups, fetch, 0)

    moves[1].wait()
    weight_line[...] = raw_weights[...].astype(F32)
    weight_copy = pltpu.make_async_copy(weight_line, weights, weight_sem)
    weight_copy.start()
    strip[...] = jnp.zeros_like(strip)
    weight_copy.wait()
    for t in range(count):
        weight_sq[tile_patch[t]] += weights[t] * weights[t]

    square = lax.broadcasted_iota(I32, (LANES, LANES), 1) - lax.broadcasted_iota(I32, (LANES, LANES), 0)
    ahead, behind = square <= -LANES // 2, square >= LANES // 2
    inner = jnp.abs(square) < LANES // 2
    segment_of = lambda axis: lax.broadcasted_iota(I32, (LANES, LANES), axis) // WARP_SEGMENT
    same_segment = segment_of(0) == segment_of(1)
    half_lanes = lax.broadcasted_iota(I32, (rows, LANES), 1) < LANES // 2
    half_row = lax.broadcasted_iota(I32, (1, LANES), 1) < LANES // 2

    def band(line, height):
        spread = jnp.broadcast_to(line, (height, LANES))
        return pltpu.roll(spread, 0, 1, stride=1, stride_axis=0)

    def line_of(offset):
        return lines[pl.ds(jnp.clip(offset + OFFSET_MAX, 0, 2 * OFFSET_MAX), 1), :]

    def arrive(g):
        pltpu.make_async_copy(tiles.at[pl.ds(0, GROUP)], raw.at[g], sems.at[g]).wait()

    def warp(g):
        slot = g & 1
        ids = [tile_at(g, j) for j in range(GROUP)]
        for j in range(0, GROUP, 2):
            spreads, ends, end_mats = [], [], []
            for i in range(2):
                circulant = band(line_of(offsets[1, ids[j + i]]), LANES)
                pick = lambda mask: jnp.where(mask, circulant, 0.0).astype(BF16)
                own = pick(inner)
                spreads.append(
                    jnp.concatenate(
                        [
                            jnp.concatenate([own, pick(ahead)], axis=1),
                            jnp.concatenate([pick(behind), own], axis=1),
                        ],
                        axis=0,
                    )
                )
                ends.append(border_columns(raw[g, j + i], WARP_SEGMENT)[0])
                end_mats.append(pick(same_segment))
            empty = jnp.zeros((LANES, LANES), BF16)
            mats = jnp.concatenate(
                [
                    jnp.concatenate([end_mats[0], empty], axis=1),
                    jnp.concatenate([empty, end_mats[1]], axis=1),
                ],
                axis=0,
            )
            mended = jnp.dot(
                jnp.concatenate(ends, axis=1), mats, preferred_element_type=F32
            ).astype(BF16)
            for i in range(2):
                value = jnp.dot(
                    side_by_side(raw[g, j + i]), spreads[i], preferred_element_type=F32
                ).astype(BF16)
                blocks = [
                    block(value[s * rows : (s + 1) * rows], b) for s in range(cols // WIDE) for b in range(2)
                ]
                blocks = mend_borders(blocks, [block(mended, i)], WARP_SEGMENT, WARP_EDGE)
                for b, piece in enumerate(blocks):
                    shifted[slot, (j + i) * rows : (j + i + 1) * rows, b * LANES : (b + 1) * LANES] = piece
        pairs = []
        for j in range(0, GROUP, 2):
            one = band(line_of(-offsets[0, ids[j]]), rows)
            two = band(pltpu.roll(line_of(-offsets[0, ids[j + 1]]), LANES // 2, 1), rows)
            pairs.append(jnp.where(half_lanes, one, two).astype(BF16))
        mixer = jnp.concatenate(pairs, axis=1)
        mixer = jnp.concatenate([mixer, mixer], axis=0)
        mixer = jnp.dot(row_mats[...], mixer, preferred_element_type=F32)
        for k in range(BASES):
            scales = [weights[t] * (coefs[k, t].astype(F32) / STEPS) for t in ids]
            scale = jnp.concatenate(
                [jnp.where(half_row, scales[j], scales[j + 1]) for j in range(0, GROUP, 2)], axis=1
            )
            mixers[slot, k * rows : (k + 1) * rows, :] = (mixer[k * rows : (k + 1) * rows] * scale).astype(BF16)

    def group_sum(g, key):
        slot = g & 1
        owner = jnp.concatenate(
            [jnp.where(half_row, key_at(g, j), key_at(g, j + 1)) for j in range(0, GROUP, 2)], axis=1
        )
        mixer = jnp.where(owner == key, mixers[slot], jnp.zeros((), BF16))
        return jnp.dot(mixer, shifted[slot], preferred_element_type=F32)

    def close(g, key, key_end):
        def one(k, carry):
            stacked[k] = total[...].astype(BF16)
            total[...] = group_sum(g, k + 1)
            return carry

        lax.fori_loop(key, key_end, one, 0)

    for move in moves[2:]:
        move.wait()
    total[...] = jnp.zeros_like(total)
    arrive(0)
    warp(0)

    def step(g, key):
        arrive(g)
        total[...] += group_sum(g - 1, key)
        warp(g)
        key_end = key_at(g, 0)
        close(g - 1, key, key_end)
        return key_end

    key = lax.fori_loop(1, groups, step, jnp.int32(0))
    total[...] += group_sum(groups - 1, key)
    close(groups - 1, key, patches)

    lane = lax.broadcasted_iota(I32, (rows, LANES), 1)
    digit_live = lane * bits < WEIGHT_BITS + 30
    scale_up = jnp.where(digit_live, power_of_two((lane + 1) * bits) * 2.0**-WEIGHT_BITS, 0.0)

    def match(q):
        mains, edges = [], []
        for k in range(BASES):
            base_k = stacked[q, k * rows : (k + 1) * rows, :]
            mains.append(side_by_side(base_k))
            edges.extend(border_columns(base_k, PSF_SEGMENT))
        edge = jnp.dot(jnp.concatenate(edges, axis=1), col_edge[...], preferred_element_type=F32)
        main = jnp.dot(jnp.concatenate(mains, axis=1), col_main[...], preferred_element_type=F32)
        blocks = [block(main[s * rows : (s + 1) * rows], b) for s in range(cols // WIDE) for b in range(2)]
        blocks = mend_borders(blocks, [block(edge, 0), block(edge, 1)], PSF_SEGMENT, PSF_EDGE)
        at = pl.ds(pl.multiple_of(HALO + q * rows, 8), rows)
        for b, piece in enumerate(blocks):
            strip[at, b * LANES : (b + 1) * LANES] = piece
        scaled = jnp.floor(weight_sq[q] * scale_up)
        strip[at, cols:] = scaled - 2.0**bits * jnp.floor(scaled * 2.0**-bits)

    batch = math.gcd(patches, PSF_BATCH)

    def match_some(i, carry):
        for j in range(batch):
            match(i * batch + j)
        return carry

    lax.fori_loop(0, patches // batch, match_some, 0)

    pairs = patches // 2
    early = first_send.shape[0]

    def hand_out(start, send, keep):
        def one(i, carry):
            d = start + i
            q = me ^ (2 * ((d + pairs // 2) % pairs) + jnp.where(d < pairs, 1, 0))
            own = pl.ds(pl.multiple_of(q * rows + helper * near, 8), near)
            other = pl.ds(pl.multiple_of(q * rows + (1 - helper) * near, 8), near)
            rounded[d] = strip[other, :].astype(BF16)
            pltpu.make_async_copy(rounded.at[d], send.at[i], out_sems.at[0]).start()
            pltpu.make_async_copy(strip.at[own], keep.at[i], out_sems.at[1]).start()
            return carry

        lax.fori_loop(0, send.shape[0], one, 0)

    hand_out(0, first_send, first_keep)
    hand_out(early, rest_send, rest_keep)
    pltpu.make_async_copy(rounded, rounded, out_sems.at[0]).wait()
    kept = strip.at[pl.ds(0, patches * near)]
    pltpu.make_async_copy(kept, kept, out_sems.at[1]).wait()


def local_stacks(patches, bits, tile_patch, weights, offsets, coefs, tiles, mats):
    count, rows, cols = tiles.shape
    near, wide = (rows + 2 * HALO) // 2, cols + LANES
    groups = -(-count // GROUP)
    hbm = pl.BlockSpec(memory_space=pltpu.HBM)
    return pl.pallas_call(
        functools.partial(stack_kernel, bits),
        out_shape=tuple(
            jax.ShapeDtypeStruct((number, near, wide), kind)
            for kind in (BF16, F32)
            for number in (patches // 4, patches - patches // 4)
        ),
        in_specs=[hbm] * (5 + len(mats)),
        out_specs=(hbm,) * 4,
        scratch_shapes=[
            pltpu.VMEM((groups, GROUP, rows, cols), BF16),
            pltpu.VMEM((2, GROUP * rows, cols), BF16),
            pltpu.VMEM((2, BASES * rows, GROUP * rows), BF16),
            pltpu.VMEM((BASES * rows, cols), F32),
            pltpu.VMEM((patches, BASES * rows, cols), BF16),
            pltpu.VMEM((patches * rows + 2 * HALO, wide), F32),
            pltpu.SemaphoreType.DMA((groups,)),
            pltpu.SMEM((count,), I32),
            pltpu.VMEM((count,), BF16),
            pltpu.SMEM(offsets.shape, I32),
            pltpu.SMEM(coefs.shape, I32),
            *(pltpu.VMEM(m.shape, m.dtype) for m in mats),
            pltpu.SemaphoreType.DMA((4 + len(mats),)),
            pltpu.VMEM((count,), F32),
            pltpu.SemaphoreType.DMA(()),
            pltpu.SMEM((count,), F32),
            pltpu.SMEM((patches,), F32),
            pltpu.SMEM((count,), I32),
            pltpu.SMEM((patches,), I32),
            pltpu.SMEM((patches,), I32),
            pltpu.VMEM((patches, near, wide), BF16),
            pltpu.SemaphoreType.DMA((2,)),
        ],
        cost_estimate=pl.CostEstimate(
            flops=2 * count * rows * cols * 4 * WIDE, bytes_accessed=count * rows * cols, transcendentals=0
        ),
        name="stacks",
    )(tile_patch, weights, offsets, coefs, tiles, *mats)


def merge_kernel(bits, *refs):
    mine = refs[-1]
    cols = mine.shape[1]
    total = refs[0][...]
    for got in refs[1:-1]:
        total = total + got[...].astype(F32)
    digits = total[:, cols:]
    lane = lax.broadcasted_iota(I32, digits.shape, 1)
    live = lane * bits < WEIGHT_BITS + 30
    value = jnp.where(live, 2.0**WEIGHT_BITS / power_of_two((lane + 1) * bits), 0.0)
    weight = jnp.sum(digits * value, axis=1, keepdims=True)
    scale = jnp.where(weight > 0.0, 1.0 / jnp.sqrt(jnp.where(weight > 0.0, weight, 1.0)), 0.0)
    mine[...] = total[:, :cols] * scale


def smooth_kernel(rows_mat, cols_mat, mine, other, coadd, detection):
    near, cols = mine.shape
    rows = coadd.shape[0]
    upper = lax.axis_index("visit") == 0
    top = jnp.where(upper, mine[...], other[...])
    bottom = jnp.where(upper, other[...], mine[...])
    coadd[: near - HALO, :] = top[HALO:]
    coadd[near - HALO :, :] = bottom[: near - HALO]
    extended = jnp.concatenate([top, bottom], axis=0).astype(BF16)
    blurred = jnp.dot(rows_mat[...], extended, preferred_element_type=F32).astype(BF16)
    blocks = cols // LANES
    window = windows([block(blurred, b) for b in range(blocks)])
    result = jnp.dot(window, cols_mat[...], preferred_element_type=F32)
    for b in range(blocks):
        detection[:, b * LANES : (b + 1) * LANES] = result[b * rows : (b + 1) * rows]


def shards(visit_tiles, tile_patch, offsets, psf_coefs, weights):
    rows, cols = visit_tiles.shape[1:]
    owners = lax.axis_size("patch")
    near = (rows + 2 * HALO) // 2
    bits = digit_bits(owners * lax.axis_size("visit"))
    mats = [jnp.asarray(m) for m in (lanczos_lines(), row_filters(rows), *psf_col_filters())]
    first_send, rest_send, first_keep, rest_keep = local_stacks(
        owners, bits, tile_patch, weights, offsets.T, psf_coefs.T, visit_tiles, mats
    )
    swap = [(0, 1), (1, 0)]
    beside = [(i, i ^ 1) for i in range(owners)]
    pairs = owners // 2
    cut = pairs // 2
    first_sum = (first_keep + lax.ppermute(first_send, "visit", swap).astype(F32)).astype(BF16)
    rest = rest_keep + lax.ppermute(rest_send, "visit", swap).astype(F32)
    evens = rest[pairs - cut :]
    bounds = sorted({0, cut // 2, cut, pairs})
    parts = [evens[cut]]
    for c, (low, high) in enumerate(zip(bounds[:-1], bounds[1:], strict=True)):
        crossing = first_sum[low:high] if high <= cut else rest[low - cut : high - cut].astype(BF16)
        crossed = lax.ppermute(crossing, "patch", beside)
        local = evens[low:high] if c == 0 else lax.optimization_barrier(evens[low:high])
        for i in range(low, high):
            e = (i + cut) % pairs
            if e == 0:
                parts.append(crossed[i - low])
            else:
                hop = [(j, j ^ (2 * e)) for j in range(owners)]
                summed = (local[i - low] + crossed[i - low].astype(F32)).astype(BF16)
                parts.append(lax.ppermute(summed, "patch", hop))
    mine = pl.pallas_call(
        functools.partial(merge_kernel, bits),
        out_shape=jax.ShapeDtypeStruct((near, cols), F32),
        compiler_params=pltpu.CompilerParams(vmem_limit_bytes=16 << 20),
        name="merge",
    )(*parts)
    other = lax.ppermute(mine, "visit", swap)
    sigma = HALO / 4.0
    out_index = np.arange(rows, dtype=np.float64)[:, None]
    in_index = np.arange(rows + 2 * HALO, dtype=np.float64)[None, :]
    rows_mat = to_bf16(gaussian(out_index + HALO - in_index, sigma, HALO))
    return pl.pallas_call(
        smooth_kernel,
        out_shape=(jax.ShapeDtypeStruct((rows, cols), F32),) * 2,
        compiler_params=pltpu.CompilerParams(vmem_limit_bytes=8 << 20),
        name="smooth",
    )(jnp.asarray(rows_mat), jnp.asarray(col_filter(sigma, HALO)), mine, other)


def solution(mesh):
    placed = (
        P(("groups", "patch", "visit"), None, None),
        P(("groups", "patch", "visit")),
        P(("groups", "patch", "visit"), None),
        P(("groups", "patch", "visit"), None),
        P(("groups", "patch", "visit")),
    )

    return jax.shard_map(
        shards,
        mesh=mesh,
        in_specs=placed,
        out_specs=(P(("groups", "patch"), None), P(("groups", "patch"), None)),
        check_vma=False,
    )
```

profile of v0, /device:TPU:0, one launch (start us, length us, event | category | flops | bytes accessed | tf_op | source)
XLA Modules:
  0.0 40.8 jit_solution(15107737751620832813)
XLA Ops:
  0.6 15.3 %stacks.1 = (bf16[2,40,1152]{2,1,0:T(8,128)(2,1)}, bf16[6,40,1152]{2,1,0:T(8,128)(2,1)}, f32[2,40,1152]{2,1,0:T(8,128)}, f32[6,40,1152]{2,1,0:T(8,128)}) custom-call(s32[56]{0:T(128)} %tile_patch_in.1, bf16[56]{0:T(256)(128)(2,1)} %raw_weights_in.1, s32[2,56]{1,0:T(2,128)} %bitcast.13, s32[3,56]{1,0:T(4,128)} %bitcast.12, bf16[56,64,1024]{2,1,0:T(8,128)(2,1)} %tiles.1, ...), custom_call_target="tpu_custom_call" | custom-call | flops 7516192768 | bytes 3670016 | tf_op jit(solution)/shard_map/stacks/pallas_call | solution.py:412
  15.9 0.0 copy-start.2
  15.9 0.6 %collective-permute-start.1 = (bf16[2,40,1152]{2,1,0:T(8,128)(2,1)}, bf16[2,40,1152]{2,1,0:T(8,128)(2,1)S(1)}, u32[]{:S(2)}, u32[]{:S(2)}) collective-permute-start(bf16[2,40,1152]{2,1,0:T(8,128)(2,1)} %get-tuple-element.9), channel_id=1, source_target_pairs={{0,1},{1,0},{2,3},{3,2},{4,5},{5,4},{6,7},{7,6},{8,9},{9,8},{10,11... | collective-permute-start | bytes 552968 | tf_op jit(solution)/shard_map/ppermute | solution.py:497
  16.5 0.1 collective-permute-start
  16.6 1.2 %collective-permute-done.1 = bf16[2,40,1152]{2,1,0:T(8,128)(2,1)S(1)} collective-permute-done((bf16[2,40,1152]{2,1,0:T(8,128)(2,1)}, bf16[2,40,1152]{2,1,0:T(8,128)(2,1)S(1)}, u32[]{:S(2)}, u32[]{:S(2)}) %collective-permute-start.1) | collective-permute-done | bytes 184352 | tf_op jit(solution)/shard_map/ppermute | solution.py:497
  17.8 1.0 %add_convert_fusion = bf16[2,40,1152]{2,1,0:T(8,128)(2,1)S(1)} fusion(f32[2,40,1152]{2,1,0:T(8,128)} %get-tuple-element.8, bf16[2,40,1152]{2,1,0:T(8,128)(2,1)S(1)} %collective-permute-done.1), kind=kLoop, calls=%fused_computation.2 | loop fusion | flops 276480 | bytes 737280 | tf_op jit(solution)/shard_map/convert_element_type | solution.py:497
  18.8 2.9 %collective-permute-start.4 = (bf16[1,40,1152]{2,1,0:T(8,128)(2,1)S(1)}, bf16[1,40,1152]{2,1,0:T(8,128)(2,1)S(1)}, u32[]{:S(2)}, u32[]{:S(2)}) collective-permute-start(bf16[1,40,1152]{2,1,0:T(8,128)(2,1)S(1)} %get-tuple-element.13), channel_id=1, source_target_pairs={{0,2},{2,0},{4,6},{6,4},{8,10},{10,8},{12,14},{14,12},{1,3},{3,1},... | collective-permute-start | bytes 276488 | tf_op jit(solution)/shard_map/ppermute | solution.py:504
  21.7 0.1 collective-permute-start.2
  21.7 0.0 collective-permute-done
  21.8 0.0 copy-done.2
  21.8 0.1 convert_add_fusion
  21.9 2.0 %collective-permute-start.6 = (bf16[2,40,1152]{2,1,0:T(8,128)(2,1)S(1)}, bf16[2,40,1152]{2,1,0:T(8,128)(2,1)S(1)}, u32[]{:S(2)}, u32[]{:S(2)}) collective-permute-start(bf16[2,40,1152]{2,1,0:T(8,128)(2,1)S(1)} %slice.70), channel_id=1, source_target_pairs={{0,2},{2,0},{4,6},{6,4},{8,10},{10,8},{12,14},{14,12},{1,3},{3,1},... | collective-permute-start | bytes 552968 | tf_op jit(solution)/shard_map/ppermute | solution.py:504
  23.9 3.3 %collective-permute-done.2 = bf16[1,40,1152]{2,1,0:T(8,128)(2,1)S(1)} collective-permute-done((bf16[1,40,1152]{2,1,0:T(8,128)(2,1)S(1)}, bf16[1,40,1152]{2,1,0:T(8,128)(2,1)S(1)}, u32[]{:S(2)}, u32[]{:S(2)}) %collective-permute-start.2) | collective-permute-done | bytes 92192 | tf_op jit(solution)/shard_map/ppermute | solution.py:504
  27.2 0.0 copy-start
  27.3 0.0 copy-start.1
  27.3 0.0 collective-permute-done.4
  27.3 4.1 %collective-permute-start.5 = (bf16[40,1152]{1,0:T(8,128)(2,1)S(1)}, bf16[40,1152]{1,0:T(8,128)(2,1)S(1)}, u32[]{:S(2)}, u32[]{:S(2)}) collective-permute-start(bf16[40,1152]{1,0:T(8,128)(2,1)S(1)} %fusion.2), channel_id=1, source_target_pairs={{0,12},{2,14},{4,8},{6,10},{8,4},{10,6},{12,0},{14,2},{1,13},{3,15... | collective-permute-start | bytes 276488 | tf_op jit(solution)/shard_map/ppermute | solution.py:513
  31.5 0.0 collective-permute-start.3
  31.5 0.0 collective-permute-done.6
  31.5 1.0 %collective-permute-start.7 = (bf16[40,1152]{1,0:T(8,128)(2,1)S(1)}, bf16[40,1152]{1,0:T(8,128)(2,1)S(1)}, u32[]{:S(2)}, u32[]{:S(2)}) collective-permute-start(bf16[40,1152]{1,0:T(8,128)(2,1)S(1)} %fusion.4), channel_id=1, source_target_pairs={{0,4},{2,6},{4,0},{6,2},{8,12},{10,14},{12,8},{14,10},{1,5},{3,7},... | collective-permute-start | bytes 276488 | tf_op jit(solution)/shard_map/ppermute | solution.py:513
  32.5 1.8 %collective-permute-done.5.refs_2_ = bf16[40,1152]{1,0:T(8,128)(2,1)S(1)} collective-permute-done((bf16[40,1152]{1,0:T(8,128)(2,1)S(1)}, bf16[40,1152]{1,0:T(8,128)(2,1)S(1)}, u32[]{:S(2)}, u32[]{:S(2)}) %collective-permute-start.5) | collective-permute-done | bytes 92192 | tf_op jit(solution)/shard_map/ppermute | solution.py:513
  34.3 3.8 %collective-permute-done.3.refs_1_ = bf16[40,1152]{1,0:T(8,128)(2,1)S(1)} collective-permute-done((bf16[40,1152]{1,0:T(8,128)(2,1)S(1)}, bf16[40,1152]{1,0:T(8,128)(2,1)S(1)}, u32[]{:S(2)}, u32[]{:S(2)}) %collective-permute-start.3) | collective-permute-done | bytes 92192 | tf_op jit(solution)/shard_map/ppermute | solution.py:513
  38.2 0.0 collective-permute-done.7.refs_4_
  38.2 0.1 merge.1.mine
  38.3 0.1 collective-permute-start.8
  38.4 1.4 %collective-permute-done.8.other = f32[40,1024]{1,0:T(8,128)S(1)} collective-permute-done((f32[40,1024]{1,0:T(8,128)S(1)}, f32[40,1024]{1,0:T(8,128)S(1)}, u32[]{:S(2)}, u32[]{:S(2)}) %collective-permute-start.8) | collective-permute-done | bytes 163872 | tf_op jit(solution)/shard_map/ppermute | solution.py:520
  39.7 0.0 copy-done
  39.8 0.0 copy-done.1
  39.8 1.1 %smooth.1 = (f32[64,1024]{1,0:T(8,128)}, f32[64,1024]{1,0:T(8,128)}) custom-call(bf16[64,80]{1,0:T(8,128)(2,1)S(1)} %copy-done.1, bf16[256,128]{1,0:T(8,128)(2,1)S(1)} %copy-done, f32[40,1024]{1,0:T(8,128)S(1)} %merge.1.mine, f32[40,1024]{1,0:T(8,128)S(1)} %collective-permute-done.8.other), custom_call_target="tpu_custom_call" | custom-call | tf_op jit(solution)/shard_map/smooth/pallas_call | solution.py:525
  (7 shorter events, 0.2 us)
Async XLA Ops:
  15.9 5.8 %copy-start.2 = (f32[6,40,1152]{2,1,0:T(8,128)S(1)}, f32[6,40,1152]{2,1,0:T(8,128)}, u32[]{:S(2)}) copy-start(f32[6,40,1152]{2,1,0:T(8,128)} %get-tuple-element.6) | copy-start | bytes 3317764
  15.9 1.8 %collective-permute-start.1 = (bf16[2,40,1152]{2,1,0:T(8,128)(2,1)}, bf16[2,40,1152]{2,1,0:T(8,128)(2,1)S(1)}, u32[]{:S(2)}, u32[]{:S(2)}) collective-permute-start(bf16[2,40,1152]{2,1,0:T(8,128)(2,1)} %get-tuple-element.9), channel_id=1, source_target_pairs={{0,1},{1,0},{2,3},{3,2},{4,5},{5,4},{6,7},{7,6},{8,9},{9,8},{10,11... | collective-permute-start | bytes 552968 | tf_op jit(solution)/shard_map/ppermute | solution.py:497
  16.5 5.3 %collective-permute-start = (bf16[6,40,1152]{2,1,0:T(8,128)(2,1)}, bf16[6,40,1152]{2,1,0:T(8,128)(2,1)S(1)}, u32[]{:S(2)}, u32[]{:S(2)}) collective-permute-start(bf16[6,40,1152]{2,1,0:T(8,128)(2,1)} %get-tuple-element.7), channel_id=1, source_target_pairs={{0,1},{1,0},{2,3},{3,2},{4,5},{5,4},{6,7},{7,6},{8,9},{9,8},{10,11... | collective-permute-start | bytes 1658888 | tf_op jit(solution)/shard_map/ppermute | solution.py:498
  18.8 8.5 %collective-permute-start.4 = (bf16[1,40,1152]{2,1,0:T(8,128)(2,1)S(1)}, bf16[1,40,1152]{2,1,0:T(8,128)(2,1)S(1)}, u32[]{:S(2)}, u32[]{:S(2)}) collective-permute-start(bf16[1,40,1152]{2,1,0:T(8,128)(2,1)S(1)} %get-tuple-element.13), channel_id=1, source_target_pairs={{0,2},{2,0},{4,6},{6,4},{8,10},{10,8},{12,14},{14,12},{1,3},{3,1},... | collective-permute-start | bytes 276488 | tf_op jit(solution)/shard_map/ppermute | solution.py:504
  21.7 5.5 %collective-permute-start.2 = (bf16[1,40,1152]{2,1,0:T(8,128)(2,1)S(1)}, bf16[1,40,1152]{2,1,0:T(8,128)(2,1)S(1)}, u32[]{:S(2)}, u32[]{:S(2)}) collective-permute-start(bf16[1,40,1152]{2,1,0:T(8,128)(2,1)S(1)} %get-tuple-element.14), channel_id=1, source_target_pairs={{0,2},{2,0},{4,6},{6,4},{8,10},{10,8},{12,14},{14,12},{1,3},{3,1},... | collective-permute-start | bytes 276488 | tf_op jit(solution)/shard_map/ppermute | solution.py:504
  21.9 9.6 %collective-permute-start.6 = (bf16[2,40,1152]{2,1,0:T(8,128)(2,1)S(1)}, bf16[2,40,1152]{2,1,0:T(8,128)(2,1)S(1)}, u32[]{:S(2)}, u32[]{:S(2)}) collective-permute-start(bf16[2,40,1152]{2,1,0:T(8,128)(2,1)S(1)} %slice.70), channel_id=1, source_target_pairs={{0,2},{2,0},{4,6},{6,4},{8,10},{10,8},{12,14},{14,12},{1,3},{3,1},... | collective-permute-start | bytes 552968 | tf_op jit(solution)/shard_map/ppermute | solution.py:504
  27.2 12.5 %copy-start = (bf16[256,128]{1,0:T(8,128)(2,1)S(1)}, bf16[256,128]{1,0:T(8,128)(2,1)}, u32[]{:S(2)}) copy-start(bf16[256,128]{1,0:T(8,128)(2,1)} %constant.17.clone.cols_mat) | copy-start | bytes 196612
  27.3 12.5 %copy-start.1 = (bf16[64,80]{1,0:T(8,128)(2,1)S(1)}, bf16[64,80]{1,0:T(8,128)(2,1)}, u32[]{:S(2)}) copy-start(bf16[64,80]{1,0:T(8,128)(2,1)} %constant.16.clone.rows_mat) | copy-start | bytes 30724
  27.3 7.0 %collective-permute-start.5 = (bf16[40,1152]{1,0:T(8,128)(2,1)S(1)}, bf16[40,1152]{1,0:T(8,128)(2,1)S(1)}, u32[]{:S(2)}, u32[]{:S(2)}) collective-permute-start(bf16[40,1152]{1,0:T(8,128)(2,1)S(1)} %fusion.2), channel_id=1, source_target_pairs={{0,12},{2,14},{4,8},{6,10},{8,4},{10,6},{12,0},{14,2},{1,13},{3,15... | collective-permute-start | bytes 276488 | tf_op jit(solution)/shard_map/ppermute | solution.py:513
  31.5 6.7 %collective-permute-start.3 = (bf16[40,1152]{1,0:T(8,128)(2,1)S(1)}, bf16[40,1152]{1,0:T(8,128)(2,1)S(1)}, u32[]{:S(2)}, u32[]{:S(2)}) collective-permute-start(bf16[40,1152]{1,0:T(8,128)(2,1)S(1)} %get-tuple-element.11), channel_id=1, source_target_pairs={{0,8},{2,10},{4,12},{6,14},{8,0},{10,2},{12,4},{14,6},{1,9},{3,11}... | collective-permute-start | bytes 276488 | tf_op jit(solution)/shard_map/ppermute | solution.py:513
  31.5 6.6 %collective-permute-start.7 = (bf16[40,1152]{1,0:T(8,128)(2,1)S(1)}, bf16[40,1152]{1,0:T(8,128)(2,1)S(1)}, u32[]{:S(2)}, u32[]{:S(2)}) collective-permute-start(bf16[40,1152]{1,0:T(8,128)(2,1)S(1)} %fusion.4), channel_id=1, source_target_pairs={{0,4},{2,6},{4,0},{6,2},{8,12},{10,14},{12,8},{14,10},{1,5},{3,7},... | collective-permute-start | bytes 276488 | tf_op jit(solution)/shard_map/ppermute | solution.py:513
  38.3 1.5 %collective-permute-start.8 = (f32[40,1024]{1,0:T(8,128)S(1)}, f32[40,1024]{1,0:T(8,128)S(1)}, u32[]{:S(2)}, u32[]{:S(2)}) collective-permute-start(f32[40,1024]{1,0:T(8,128)S(1)} %merge.1.mine), channel_id=1, source_target_pairs={{0,1},{1,0},{2,3},{3,2},{4,5},{5,4},{6,7},{7,6},{8,9},{9,8},{10,11... | collective-permute-start | bytes 491528 | tf_op jit(solution)/shard_map/ppermute | solution.py:520
where the time goes:
time: 41 us; the launch traced here: 40.8 us
  Pallas kernels  16.5 us (40%)
  waiting for transfers between devices  11.5 us (28%)
  starting transfers between devices  10.8 us (26%)
  other arithmetic  1.21 us (3%)
  between operations  0.74 us (2%)
    pallas_call x1, Pallas kernels, local_stacks(): pl.pallas_call(functools.partial(stack_kernel, bits), out_shape=tuple((ja...  15.3 us
    ppermute x3, waiting for transfers between devices, shards(): parts.append(lax.ppermute(summed, 'patch', hop))  5.63 us
    ppermute x3, starting transfers between devices, shards(): parts.append(lax.ppermute(summed, 'patch', hop))  5.14 us
    ppermute x3, starting transfers between devices, shards(): crossed = lax.ppermute(crossing, 'patch', beside)  4.95 us
    ppermute x3, waiting for transfers between devices, shards(): crossed = lax.ppermute(crossing, 'patch', beside)  3.31 us
    ppermute x1, waiting for transfers between devices, shards(): other = lax.ppermute(mine, 'visit', swap)  1.38 us
    ppermute x1, waiting for transfers between devices, shards(): lax.ppermute(first_send, 'visit', swap).astype(F32)  1.19 us
    pallas_call x1, Pallas kernels, shards(): pl.pallas_call(smooth_kernel, out_shape=(jax.ShapeDtypeStruct((rows, cols...  1.06 us
  transfers between devices with their start and end apart: 9, of which 5 were waited for; matrix products, arithmetic and copies ran while one was open for 3% of the time, Pallas kernels for 0%

commit v1 on v0

--- a/solution.py
+++ b/solution.py
@@ -19,6 +19,7 @@
 WIDE = 2 * LANES
 GROUP = 4
 PSF_BATCH = 4
+DEFERRED = 16
 STEPS = 64
 OFFSET_MAX = 128
 WEIGHT_BITS = 10
@@ -170,18 +171,18 @@
     weight_line,
     weight_sem,
     weights,
-    weight_sq,
+    patch_line,
     order,
-    first,
     cursor,
-    rounded,
-    out_sems,
 ):
     me = lax.axis_index("patch")
     helper = lax.axis_index("visit")
     count, rows, cols = tiles.shape
-    patches = stacked.shape[0]
-    near = (rows + 2 * HALO) // 2
+    patches = cursor.shape[0]
+    deferred = stacked.shape[0] == patches
+    blocks = cols // LANES
+    stripes = rows // 8
+    near = (stripes + 2) // 2
 
     moves = [
         pltpu.make_async_copy(source, target, in_sems.at[i])
@@ -189,6 +190,7 @@
             (
                 (tile_patch_in, tile_patch),
                 (raw_weights_in, raw_weights),
+                (tile_patch_in, patch_line),
                 (offsets_in, offsets),
                 (coefs_in, coefs),
                 (lines_in, lines),
@@ -202,14 +204,12 @@
         move.start()
     for k in range(patches):
         cursor[k] = 0
-        weight_sq[k] = 0.0
     moves[0].wait()
     for t in range(count):
         cursor[tile_patch[t]] += 1
     running = 0
     for k in range(patches):
         number = cursor[k]
-        first[k] = running
         cursor[k] = running
         running = running + number
     for t in range(count):
@@ -239,10 +239,9 @@
     weight_line[...] = raw_weights[...].astype(F32)
     weight_copy = pltpu.make_async_copy(weight_line, weights, weight_sem)
     weight_copy.start()
-    strip[...] = jnp.zeros_like(strip)
+    strip[:blocks] = jnp.zeros((blocks, 8, LANES), F32)
+    strip[strip.shape[0] - blocks :] = jnp.zeros((blocks, 8, LANES), F32)
     weight_copy.wait()
-    for t in range(count):
-        weight_sq[tile_patch[t]] += weights[t] * weights[t]
 
     square = lax.broadcasted_iota(I32, (LANES, LANES), 1) - lax.broadcasted_iota(I32, (LANES, LANES), 0)
     ahead, behind = square <= -LANES // 2, square >= LANES // 2
@@ -326,10 +325,37 @@
         mixer = jnp.where(owner == key, mixers[slot], jnp.zeros((), BF16))
         return jnp.dot(mixer, shifted[slot], preferred_element_type=F32)
 
+    def match(q):
+        mains, edges = [], []
+        for k in range(BASES):
+            base_k = stacked[q if deferred else 0, k * rows : (k + 1) * rows, :]
+            mains.append(side_by_side(base_k))
+            edges.extend(border_columns(base_k, PSF_SEGMENT))
+        edge = jnp.dot(jnp.concatenate(edges, axis=1), col_edge[...], preferred_element_type=F32)
+        main = jnp.dot(jnp.concatenate(mains, axis=1), col_main[...], preferred_element_type=F32)
+        pieces = [block(main[s * rows : (s + 1) * rows], b) for s in range(cols // WIDE) for b in range(2)]
+        pieces = mend_borders(pieces, [block(edge, 0), block(edge, 1)], PSF_SEGMENT, PSF_EDGE)
+        for b, piece in enumerate(pieces):
+            for i in range(stripes):
+                strip[(q * stripes + i + 1) * blocks + b] = piece[8 * i : 8 * i + 8]
+
     def close(g, key, key_end):
         def one(k, carry):
-            stacked[k] = total[...].astype(BF16)
-            total[...] = group_sum(g, k + 1)
+            if deferred:
+                stacked[k] = total[...].astype(BF16)
+            else:
+                stacked[0] = total[...].astype(BF16)
+                match(k)
+            goes_on = cursor[k] < jnp.minimum((g + 1) * GROUP, count)
+
+            @pl.when(goes_on)
+            def _():
+                total[...] = group_sum(g, k + 1)
+
+            @pl.when(jnp.logical_not(goes_on))
+            def _():
+                total[...] = jnp.zeros_like(total)
+
             return carry
 
         lax.fori_loop(key, key_end, one, 0)
@@ -352,26 +378,6 @@
     total[...] += group_sum(groups - 1, key)
     close(groups - 1, key, patches)
 
-    lane = lax.broadcasted_iota(I32, (rows, LANES), 1)
-    digit_live = lane * bits < WEIGHT_BITS + 30
-    scale_up = jnp.where(digit_live, power_of_two((lane + 1) * bits) * 2.0**-WEIGHT_BITS, 0.0)
-
-    def match(q):
-        mains, edges = [], []
-        for k in range(BASES):
-            base_k = stacked[q, k * rows : (k + 1) * rows, :]
-            mains.append(side_by_side(base_k))
-            edges.extend(border_columns(base_k, PSF_SEGMENT))
-        edge = jnp.dot(jnp.concatenate(edges, axis=1), col_edge[...], preferred_element_type=F32)
-        main = jnp.dot(jnp.concatenate(mains, axis=1), col_main[...], preferred_element_type=F32)
-        blocks = [block(main[s * rows : (s + 1) * rows], b) for s in range(cols // WIDE) for b in range(2)]
-        blocks = mend_borders(blocks, [block(edge, 0), block(edge, 1)], PSF_SEGMENT, PSF_EDGE)
-        at = pl.ds(pl.multiple_of(HALO + q * rows, 8), rows)
-        for b, piece in enumerate(blocks):
-            strip[at, b * LANES : (b + 1) * LANES] = piece
-        scaled = jnp.floor(weight_sq[q] * scale_up)
-        strip[at, cols:] = scaled - 2.0**bits * jnp.floor(scaled * 2.0**-bits)
-
     batch = math.gcd(patches, PSF_BATCH)
 
     def match_some(i, carry):
@@ -379,89 +385,122 @@
             match(i * batch + j)
         return carry
 
-    lax.fori_loop(0, patches // batch, match_some, 0)
+    if deferred:
+        lax.fori_loop(0, patches // batch, match_some, 0)
 
     pairs = patches // 2
     early = first_send.shape[0]
+    tile_row = lax.broadcasted_iota(I32, (8, LANES), 0)
+    tile_lane = lax.broadcasted_iota(I32, (8, LANES), 1)
+    digit_live = tile_lane * bits < WEIGHT_BITS + 30
+    scale_up = jnp.where(digit_live, power_of_two((tile_lane + 1) * bits) * 2.0**-WEIGHT_BITS, 0.0)
+    line = patch_line[...].reshape(1, count)
+    squares = weight_line[...].reshape(1, count)
+    squares = squares * squares
+
+    def weight_digits(q, side):
+        patch = jnp.where(tile_row[:, :1] == 0, q, q + side)
+        mine = (line == patch) & (tile_row[:, :1] < 2)
+        scaled = jnp.floor(jnp.sum(jnp.where(mine, squares, 0.0), axis=1, keepdims=True) * scale_up)
+        return scaled - 2.0**bits * jnp.floor(scaled * 2.0**-bits)
 
     def hand_out(start, send, keep):
         def one(i, carry):
             d = start + i
             q = me ^ (2 * ((d + pairs // 2) % pairs) + jnp.where(d < pairs, 1, 0))
-            own = pl.ds(pl.multiple_of(q * rows + helper * near, 8), near)
-            other = pl.ds(pl.multiple_of(q * rows + (1 - helper) * near, 8), near)
-            rounded[d] = strip[other, :].astype(BF16)
-            pltpu.make_async_copy(rounded.at[d], send.at[i], out_sems.at[0]).start()
-            pltpu.make_async_copy(strip.at[own], keep.at[i], out_sems.at[1]).start()
+            body = near * blocks
+            own = pl.ds((q * stripes + helper * near) * blocks, body)
+            other = pl.ds((q * stripes + (1 - helper) * near) * blocks, body)
+            send[i, :body] = strip[other].astype(BF16)
+            send[i, body] = weight_digits(q, 1 - 2 * helper).astype(BF16)
+            keep[i, :body] = strip[own]
+            keep[i, body] = weight_digits(q, 2 * helper - 1)
             return carry
 
         lax.fori_loop(0, send.shape[0], one, 0)
 
     hand_out(0, first_send, first_keep)
     hand_out(early, rest_send, rest_keep)
-    pltpu.make_async_copy(rounded, rounded, out_sems.at[0]).wait()
-    kept = strip.at[pl.ds(0, patches * near)]
-    pltpu.make_async_copy(kept, kept, out_sems.at[1]).wait()
+
+
+def message_tiles(rows, cols):
+    return (rows // 8 + 2) // 2 * (cols // LANES) + 1
 
 
 def local_stacks(patches, bits, tile_patch, weights, offsets, coefs, tiles, mats):
     count, rows, cols = tiles.shape
-    near, wide = (rows + 2 * HALO) // 2, cols + LANES
+    blocks = cols // LANES
+    message = message_tiles(rows, cols)
     groups = -(-count // GROUP)
     hbm = pl.BlockSpec(memory_space=pltpu.HBM)
     return pl.pallas_call(
         functools.partial(stack_kernel, bits),
         out_shape=tuple(
-            jax.ShapeDtypeStruct((number, near, wide), kind)
+            jax.ShapeDtypeStruct((number, message, 8, LANES), kind)
             for kind in (BF16, F32)
             for number in (patches // 4, patches - patches // 4)
         ),
         in_specs=[hbm] * (5 + len(mats)),
-        out_specs=(hbm,) * 4,
+        out_specs=(pl.BlockSpec(memory_space=pltpu.VMEM),) * 4,
         scratch_shapes=[
             pltpu.VMEM((groups, GROUP, rows, cols), BF16),
             pltpu.VMEM((2, GROUP * rows, cols), BF16),
             pltpu.VMEM((2, BASES * rows, GROUP * rows), BF16),
             pltpu.VMEM((BASES * rows, cols), F32),
-            pltpu.VMEM((patches, BASES * rows, cols), BF16),
-            pltpu.VMEM((patches * rows + 2 * HALO, wide), F32),
+            pltpu.VMEM((patches if patches <= DEFERRED else 1, BASES * rows, cols), BF16),
+            pltpu.VMEM(((patches * rows // 8 + 2) * blocks, 8, LANES), F32),
             pltpu.SemaphoreType.DMA((groups,)),
             pltpu.SMEM((count,), I32),
             pltpu.VMEM((count,), BF16),
             pltpu.SMEM(offsets.shape, I32),
             pltpu.SMEM(coefs.shape, I32),
             *(pltpu.VMEM(m.shape, m.dtype) for m in mats),
-            pltpu.SemaphoreType.DMA((4 + len(mats),)),
+            pltpu.SemaphoreType.DMA((5 + len(mats),)),
             pltpu.VMEM((count,), F32),
             pltpu.SemaphoreType.DMA(()),
             pltpu.SMEM((count,), F32),
-            pltpu.SMEM((patches,), F32),
+            pltpu.VMEM((count,), I32),
             pltpu.SMEM((count,), I32),
             pltpu.SMEM((patches,), I32),
-            pltpu.SMEM((patches,), I32),
-            pltpu.VMEM((patches, near, wide), BF16),
-            pltpu.SemaphoreType.DMA((2,)),
         ],
         cost_estimate=pl.CostEstimate(
             flops=2 * count * rows * cols * 4 * WIDE, bytes_accessed=count * rows * cols, transcendentals=0
         ),
+        compiler_params=pltpu.CompilerParams(vmem_limit_bytes=48 << 20),
         name="stacks",
-    )(tile_patch, weights, offsets, coefs, tiles, *mats)
+    )(*(pltpu.with_memory_space_constraint(a, pltpu.HBM) for a in (tile_patch, weights, offsets, coefs, tiles, *mats)))
+
+
+def add_kernel(keep, got, *outs):
+    start = 0
+    for out in outs:
+        at = slice(start, start + out.shape[0])
+        out[...] = (keep[at] + got[at].astype(F32)).astype(BF16)
+        start += out.shape[0]
 
 
 def merge_kernel(bits, *refs):
     mine = refs[-1]
-    cols = mine.shape[1]
+    near, cols = mine.shape
+    blocks = cols // LANES
     total = refs[0][...]
     for got in refs[1:-1]:
         total = total + got[...].astype(F32)
-    digits = total[:, cols:]
-    lane = lax.broadcasted_iota(I32, digits.shape, 1)
+    lane = lax.broadcasted_iota(I32, (8, LANES), 1)
     live = lane * bits < WEIGHT_BITS + 30
     value = jnp.where(live, 2.0**WEIGHT_BITS / power_of_two((lane + 1) * bits), 0.0)
-    weight = jnp.sum(digits * value, axis=1, keepdims=True)
+    weight = jnp.sum(total[-1] * value, axis=1, keepdims=True)
     scale = jnp.where(weight > 0.0, 1.0 / jnp.sqrt(jnp.where(weight > 0.0, weight, 1.0)), 0.0)
-    mine[...] = total[:, :cols] * scale
+    inner, outer = scale[0:1], scale[1:2]
+    upper = lax.axis_index("visit") == 0
+    for i in range(near // 8):
+        here = inner
+        if i == 0:
+            here = jnp.where(upper, outer, inner)
+        elif i == near // 8 - 1:
+            here = jnp.where(upper, inner, outer)
+        for b in range(blocks):
+            mine[8 * i : 8 * i + 8, b * LANES : (b + 1) * LANES] = total[i * blocks + b] * here
 
 
 def smooth_kernel(rows_mat, cols_mat, mine, other, coadd, detection):
@@ -494,13 +533,22 @@
     beside = [(i, i ^ 1) for i in range(owners)]
     pairs = owners // 2
     cut = pairs // 2
-    first_sum = (first_keep + lax.ppermute(first_send, "visit", swap).astype(F32)).astype(BF16)
+    bounds = sorted({0, cut // 2, cut, pairs})
+    first_got = lax.ppermute(first_send, "visit", swap)
+    first_sums = pl.pallas_call(
+        add_kernel,
+        out_shape=tuple(
+            jax.ShapeDtypeStruct((high - low, *first_keep.shape[1:]), BF16)
+            for low, high in zip(bounds[:-2], bounds[1:-1], strict=True)
+        ),
+        compiler_params=pltpu.CompilerParams(vmem_limit_bytes=16 << 20),
+        name="add",
+    )(first_keep, first_got)
     rest = rest_keep + lax.ppermute(rest_send, "visit", swap).astype(F32)
     evens = rest[pairs - cut :]
-    bounds = sorted({0, cut // 2, cut, pairs})
     parts = [evens[cut]]
     for c, (low, high) in enumerate(zip(bounds[:-1], bounds[1:], strict=True)):
-        crossing = first_sum[low:high] if high <= cut else rest[low - cut : high - cut].astype(BF16)
+        crossing = first_sums[c] if high <= cut else rest[low - cut : high - cut].astype(BF16)
         crossed = lax.ppermute(crossing, "patch", beside)
         local = evens[low:high] if c == 0 else lax.optimization_barrier(evens[low:high])
         for i in range(low, high):

time: 41 us -> 38.4 us (0.937)
  Pallas kernels: 16.5 us -> 15.4 us
  other arithmetic: 1.21 us -> 0.21 us
    pallas_call x1, Pallas kernels: 15.3 us -> 14.1 us  [local_stacks(): pl.pallas_call(functools.partial(stack_kernel, bits), out_shape=tuple((ja...]
    convert_element_type x1 -> x0, other arithmetic: 1.03 us -> none  [shards(): (first_keep + lax.ppermute(first_send, 'visit', swap).astype(F32)).astype...]
    ppermute x1, starting transfers between devices: 0.57 us -> 0.08 us  [shards(): first_got = lax.ppermute(first_send, 'visit', swap)]
    ppermute x1, starting transfers between devices: 0.08 us -> 0.56 us  [shards(): rest = rest_keep + lax.ppermute(rest_send, 'visit', swap).astype(F32)]
    ppermute x1, waiting for transfers between devices: 1.19 us -> 1.67 us  [shards(): first_got = lax.ppermute(first_send, 'visit', swap)]
    ppermute x3, waiting for transfers between devices: 5.63 us -> 5.15 us  [shards(): parts.append(lax.ppermute(summed, 'patch', hop))]
  transfers between devices with their start and end apart: 9 -> 9, of which waited for: 5 -> 6; matrix products, arithmetic and copies ran while one was open for 3% -> 1% of each run, Pallas kernels for 0% -> 0%
where the time goes in v1:
time: 38.4 us; the launch traced here: 38.2 us
  Pallas kernels  15.4 us (40%)
  waiting for transfers between devices  11.2 us (29%)
  starting transfers between devices  10.6 us (28%)
  between operations  0.71 us (2%)
    pallas_call x1, Pallas kernels, local_stacks(): pl.pallas_call(functools.partial(stack_kernel, bits), out_shape=tuple((ja...  14.1 us
    ppermute x3, waiting for transfers between devices, shards(): parts.append(lax.ppermute(summed, 'patch', hop))  5.15 us
    ppermute x3, starting transfers between devices, shards(): parts.append(lax.ppermute(summed, 'patch', hop))  5.08 us
    ppermute x3, starting transfers between devices, shards(): crossed = lax.ppermute(crossing, 'patch', beside)  4.77 us
    ppermute x3, waiting for transfers between devices, shards(): crossed = lax.ppermute(crossing, 'patch', beside)  3.04 us
    ppermute x1, waiting for transfers between devices, shards(): first_got = lax.ppermute(first_send, 'visit', swap)  1.67 us
    ppermute x1, waiting for transfers between devices, shards(): other = lax.ppermute(mine, 'visit', swap)  1.38 us
    pallas_call x1, Pallas kernels, shards(): pl.pallas_call(smooth_kernel, out_shape=(jax.ShapeDtypeStruct((rows, cols...  1.06 us
  transfers between devices with their start and end apart: 9, of which 6 were waited for; matrix products, arithmetic and copies ran while one was open for 1% of the time, Pallas kernels for 0%

profile of v1, /device:TPU:0, one launch (start us, length us, event | category | flops | bytes accessed | tf_op | source)
XLA Modules:
  0.0 38.2 jit_solution(14397068167876971663)
XLA Ops:
  0.6 0.0 copy-start
  0.6 0.0 copy-start.1
  0.7 14.1 %stacks.1 = (bf16[2,41,8,128]{3,2,1,0:T(8,128)(2,1)S(1)}, bf16[6,41,8,128]{3,2,1,0:T(8,128)(2,1)S(1)}, f32[2,41,8,128]{3,2,1,0:T(8,128)S(1)}, f32[6,41,8,128]{3,2,1,0:T(8,128)S(1)}) custom-call(s32[56]{0:T(128)} %tile_patch_in.1, bf16[56]{0:T(256)(128)(2,1)} %raw_weights_in.1, s32[2,56]{1,0:T(2,128)} %bitcast.13, s32[3,56]{1,0:T(4,128)} %bitcast.12, ...), custom_call_target="tpu_custom_call" | custom-call | flops 7516192768 | bytes 3670016 | tf_op jit(solution)/shard_map/stacks/pallas_call | solution.py:436
  14.8 0.6 %collective-permute-start = (bf16[6,41,8,128]{3,2,1,0:T(8,128)(2,1)S(1)}, bf16[6,41,8,128]{3,2,1,0:T(8,128)(2,1)S(1)}, u32[]{:S(2)}, u32[]{:S(2)}) collective-permute-start(bf16[6,41,8,128]{3,2,1,0:T(8,128)(2,1)S(1)} %get-tuple-element.9), channel_id=1, source_target_pairs={{0,1},{1,0},{2,3},{3,2},{4,5},{5,4},{6,7},{7,6},{8,9},{9,8},{10,11... | collective-permute-start | bytes 1511432 | tf_op jit(solution)/shard_map/ppermute | solution.py:547
  15.4 0.1 collective-permute-start.1
  15.4 1.7 %collective-permute-done.1.got = bf16[2,41,8,128]{3,2,1,0:T(8,128)(2,1)S(1)} collective-permute-done((bf16[2,41,8,128]{3,2,1,0:T(8,128)(2,1)S(1)}, bf16[2,41,8,128]{3,2,1,0:T(8,128)(2,1)S(1)}, u32[]{:S(2)}, u32[]{:S(2)}) %collective-permute-start.1) | collective-permute-done | bytes 167968 | tf_op jit(solution)/shard_map/ppermute | solution.py:537
  17.2 2.7 %collective-permute-start.2 = (bf16[1,41,8,128]{3,2,1,0:T(8,128)(2,1)S(1)}, bf16[1,41,8,128]{3,2,1,0:T(8,128)(2,1)S(1)}, u32[]{:S(2)}, u32[]{:S(2)}) collective-permute-start(bf16[1,41,8,128]{3,2,1,0:T(8,128)(2,1)S(1)} %get-tuple-element.12), channel_id=1, source_target_pairs={{0,2},{2,0},{4,6},{6,4},{8,10},{10,8},{12,14},{14,12},{1,3},{3,1},... | collective-permute-start | bytes 251912 | tf_op jit(solution)/shard_map/ppermute | solution.py:552
  19.8 0.1 collective-permute-start.4
  19.9 0.0 collective-permute-done
  19.9 0.1 convert_add_fusion
  20.1 2.0 %collective-permute-start.6 = (bf16[2,41,8,128]{3,2,1,0:T(8,128)(2,1)S(1)}, bf16[2,41,8,128]{3,2,1,0:T(8,128)(2,1)S(1)}, u32[]{:S(2)}, u32[]{:S(2)}) collective-permute-start(bf16[2,41,8,128]{3,2,1,0:T(8,128)(2,1)S(1)} %slice.60), channel_id=1, source_target_pairs={{0,2},{2,0},{4,6},{6,4},{8,10},{10,8},{12,14},{14,12},{1,3},{3,1},... | collective-permute-start | bytes 503816 | tf_op jit(solution)/shard_map/ppermute | solution.py:552
  22.1 0.9 %collective-permute-done.2 = bf16[1,41,8,128]{3,2,1,0:T(8,128)(2,1)S(1)} collective-permute-done((bf16[1,41,8,128]{3,2,1,0:T(8,128)(2,1)S(1)}, bf16[1,41,8,128]{3,2,1,0:T(8,128)(2,1)S(1)}, u32[]{:S(2)}, u32[]{:S(2)}) %collective-permute-start.2) | collective-permute-done | bytes 84000 | tf_op jit(solution)/shard_map/ppermute | solution.py:552
  23.0 2.2 %collective-permute-done.4 = bf16[1,41,8,128]{3,2,1,0:T(8,128)(2,1)S(1)} collective-permute-done((bf16[1,41,8,128]{3,2,1,0:T(8,128)(2,1)S(1)}, bf16[1,41,8,128]{3,2,1,0:T(8,128)(2,1)S(1)}, u32[]{:S(2)}, u32[]{:S(2)}) %collective-permute-start.4) | collective-permute-done | bytes 84000 | tf_op jit(solution)/shard_map/ppermute | solution.py:552
  25.2 4.1 %collective-permute-start.5 = (bf16[41,8,128]{2,1,0:T(8,128)(2,1)S(1)}, bf16[41,8,128]{2,1,0:T(8,128)(2,1)S(1)}, u32[]{:S(2)}, u32[]{:S(2)}) collective-permute-start(bf16[41,8,128]{2,1,0:T(8,128)(2,1)S(1)} %fusion.2), channel_id=1, source_target_pairs={{0,12},{2,14},{4,8},{6,10},{8,4},{10,6},{12,0},{14,2},{1,13},{3,15... | collective-permute-start | bytes 251912 | tf_op jit(solution)/shard_map/ppermute | solution.py:561
  29.3 0.0 collective-permute-start.3
  29.3 0.0 collective-permute-done.6
  29.4 1.0 %collective-permute-start.7 = (bf16[41,8,128]{2,1,0:T(8,128)(2,1)S(1)}, bf16[41,8,128]{2,1,0:T(8,128)(2,1)S(1)}, u32[]{:S(2)}, u32[]{:S(2)}) collective-permute-start(bf16[41,8,128]{2,1,0:T(8,128)(2,1)S(1)} %fusion.4), channel_id=1, source_target_pairs={{0,4},{2,6},{4,0},{6,2},{8,12},{10,14},{12,8},{14,10},{1,5},{3,7},... | collective-permute-start | bytes 251912 | tf_op jit(solution)/shard_map/ppermute | solution.py:561
  30.3 1.7 %collective-permute-done.5.refs_2_ = bf16[41,8,128]{2,1,0:T(8,128)(2,1)S(1)} collective-permute-done((bf16[41,8,128]{2,1,0:T(8,128)(2,1)S(1)}, bf16[41,8,128]{2,1,0:T(8,128)(2,1)S(1)}, u32[]{:S(2)}, u32[]{:S(2)}) %collective-permute-start.5) | collective-permute-done | bytes 84000 | tf_op jit(solution)/shard_map/ppermute | solution.py:561
  32.0 3.5 %collective-permute-done.3.refs_1_ = bf16[41,8,128]{2,1,0:T(8,128)(2,1)S(1)} collective-permute-done((bf16[41,8,128]{2,1,0:T(8,128)(2,1)S(1)}, bf16[41,8,128]{2,1,0:T(8,128)(2,1)S(1)}, u32[]{:S(2)}, u32[]{:S(2)}) %collective-permute-start.3) | collective-permute-done | bytes 84000 | tf_op jit(solution)/shard_map/ppermute | solution.py:561
  35.5 0.0 collective-permute-done.7.refs_4_
  35.5 0.2 merge.1.mine
  35.7 0.1 collective-permute-start.8
  35.8 1.4 %collective-permute-done.8.other = f32[40,1024]{1,0:T(8,128)S(1)} collective-permute-done((f32[40,1024]{1,0:T(8,128)S(1)}, f32[40,1024]{1,0:T(8,128)S(1)}, u32[]{:S(2)}, u32[]{:S(2)}) %collective-permute-start.8) | collective-permute-done | bytes 163872 | tf_op jit(solution)/shard_map/ppermute | solution.py:568
  37.2 0.0 copy-done
  37.2 0.0 copy-done.1
  37.2 1.1 %smooth.1 = (f32[64,1024]{1,0:T(8,128)}, f32[64,1024]{1,0:T(8,128)}) custom-call(bf16[64,80]{1,0:T(8,128)(2,1)S(1)} %copy-done.1, bf16[256,128]{1,0:T(8,128)(2,1)S(1)} %copy-done, f32[40,1024]{1,0:T(8,128)S(1)} %merge.1.mine, f32[40,1024]{1,0:T(8,128)S(1)} %collective-permute-done.8.other), custom_call_target="tpu_custom_call" | custom-call | tf_op jit(solution)/shard_map/smooth/pallas_call | solution.py:573
  (7 shorter events, 0.2 us)
Async XLA Ops:
  0.6 36.5 %copy-start = (bf16[256,128]{1,0:T(8,128)(2,1)S(1)}, bf16[256,128]{1,0:T(8,128)(2,1)}, u32[]{:S(2)}) copy-start(bf16[256,128]{1,0:T(8,128)(2,1)} %constant.17.clone.cols_mat) | copy-start | bytes 196612
  0.6 36.5 %copy-start.1 = (bf16[64,80]{1,0:T(8,128)(2,1)S(1)}, bf16[64,80]{1,0:T(8,128)(2,1)}, u32[]{:S(2)}) copy-start(bf16[64,80]{1,0:T(8,128)(2,1)} %constant.16.clone.rows_mat) | copy-start | bytes 30724
  14.8 5.1 %collective-permute-start = (bf16[6,41,8,128]{3,2,1,0:T(8,128)(2,1)S(1)}, bf16[6,41,8,128]{3,2,1,0:T(8,128)(2,1)S(1)}, u32[]{:S(2)}, u32[]{:S(2)}) collective-permute-start(bf16[6,41,8,128]{3,2,1,0:T(8,128)(2,1)S(1)} %get-tuple-element.9), channel_id=1, source_target_pairs={{0,1},{1,0},{2,3},{3,2},{4,5},{5,4},{6,7},{7,6},{8,9},{9,8},{10,11... | collective-permute-start | bytes 1511432 | tf_op jit(solution)/shard_map/ppermute | solution.py:547
  15.4 1.7 %collective-permute-start.1 = (bf16[2,41,8,128]{3,2,1,0:T(8,128)(2,1)S(1)}, bf16[2,41,8,128]{3,2,1,0:T(8,128)(2,1)S(1)}, u32[]{:S(2)}, u32[]{:S(2)}) collective-permute-start(bf16[2,41,8,128]{3,2,1,0:T(8,128)(2,1)S(1)} %get-tuple-element.11), channel_id=1, source_target_pairs={{0,1},{1,0},{2,3},{3,2},{4,5},{5,4},{6,7},{7,6},{8,9},{9,8},{10,11... | collective-permute-start | bytes 503816 | tf_op jit(solution)/shard_map/ppermute | solution.py:537
  17.2 5.8 %collective-permute-start.2 = (bf16[1,41,8,128]{3,2,1,0:T(8,128)(2,1)S(1)}, bf16[1,41,8,128]{3,2,1,0:T(8,128)(2,1)S(1)}, u32[]{:S(2)}, u32[]{:S(2)}) collective-permute-start(bf16[1,41,8,128]{3,2,1,0:T(8,128)(2,1)S(1)} %get-tuple-element.12), channel_id=1, source_target_pairs={{0,2},{2,0},{4,6},{6,4},{8,10},{10,8},{12,14},{14,12},{1,3},{3,1},... | collective-permute-start | bytes 251912 | tf_op jit(solution)/shard_map/ppermute | solution.py:552
  19.8 5.4 %collective-permute-start.4 = (bf16[1,41,8,128]{3,2,1,0:T(8,128)(2,1)S(1)}, bf16[1,41,8,128]{3,2,1,0:T(8,128)(2,1)S(1)}, u32[]{:S(2)}, u32[]{:S(2)}) collective-permute-start(bf16[1,41,8,128]{3,2,1,0:T(8,128)(2,1)S(1)} %get-tuple-element.13), channel_id=1, source_target_pairs={{0,2},{2,0},{4,6},{6,4},{8,10},{10,8},{12,14},{14,12},{1,3},{3,1},... | collective-permute-start | bytes 251912 | tf_op jit(solution)/shard_map/ppermute | solution.py:552
  20.1 9.3 %collective-permute-start.6 = (bf16[2,41,8,128]{3,2,1,0:T(8,128)(2,1)S(1)}, bf16[2,41,8,128]{3,2,1,0:T(8,128)(2,1)S(1)}, u32[]{:S(2)}, u32[]{:S(2)}) collective-permute-start(bf16[2,41,8,128]{3,2,1,0:T(8,128)(2,1)S(1)} %slice.60), channel_id=1, source_target_pairs={{0,2},{2,0},{4,6},{6,4},{8,10},{10,8},{12,14},{14,12},{1,3},{3,1},... | collective-permute-start | bytes 503816 | tf_op jit(solution)/shard_map/ppermute | solution.py:552
  25.2 6.8 %collective-permute-start.5 = (bf16[41,8,128]{2,1,0:T(8,128)(2,1)S(1)}, bf16[41,8,128]{2,1,0:T(8,128)(2,1)S(1)}, u32[]{:S(2)}, u32[]{:S(2)}) collective-permute-start(bf16[41,8,128]{2,1,0:T(8,128)(2,1)S(1)} %fusion.2), channel_id=1, source_target_pairs={{0,12},{2,14},{4,8},{6,10},{8,4},{10,6},{12,0},{14,2},{1,13},{3,15... | collective-permute-start | bytes 251912 | tf_op jit(solution)/shard_map/ppermute | solution.py:561
  29.3 6.2 %collective-permute-start.3 = (bf16[41,8,128]{2,1,0:T(8,128)(2,1)S(1)}, bf16[41,8,128]{2,1,0:T(8,128)(2,1)S(1)}, u32[]{:S(2)}, u32[]{:S(2)}) collective-permute-start(bf16[41,8,128]{2,1,0:T(8,128)(2,1)S(1)} %get-tuple-element.15), channel_id=1, source_target_pairs={{0,8},{2,10},{4,12},{6,14},{8,0},{10,2},{12,4},{14,6},{1,9},{3,11}... | collective-permute-start | bytes 251912 | tf_op jit(solution)/shard_map/ppermute | solution.py:561
  29.4 6.1 %collective-permute-start.7 = (bf16[41,8,128]{2,1,0:T(8,128)(2,1)S(1)}, bf16[41,8,128]{2,1,0:T(8,128)(2,1)S(1)}, u32[]{:S(2)}, u32[]{:S(2)}) collective-permute-start(bf16[41,8,128]{2,1,0:T(8,128)(2,1)S(1)} %fusion.4), channel_id=1, source_target_pairs={{0,4},{2,6},{4,0},{6,2},{8,12},{10,14},{12,8},{14,10},{1,5},{3,7},... | collective-permute-start | bytes 251912 | tf_op jit(solution)/shard_map/ppermute | solution.py:561
  35.7 1.5 %collective-permute-start.8 = (f32[40,1024]{1,0:T(8,128)S(1)}, f32[40,1024]{1,0:T(8,128)S(1)}, u32[]{:S(2)}, u32[]{:S(2)}) collective-permute-start(f32[40,1024]{1,0:T(8,128)S(1)} %merge.1.mine), channel_id=1, source_target_pairs={{0,1},{1,0},{2,3},{3,2},{4,5},{5,4},{6,7},{7,6},{8,9},{9,8},{10,11... | collective-permute-start | bytes 491528 | tf_op jit(solution)/shard_map/ppermute | solution.py:568

commit v2 on v1

--- a/solution.py
+++ b/solution.py
@@ -179,7 +179,7 @@
     helper = lax.axis_index("visit")
     count, rows, cols = tiles.shape
     patches = cursor.shape[0]
-    deferred = stacked.shape[0] == patches
+    deferred = total.shape[0] == patches
     blocks = cols // LANES
     stripes = rows // 8
     near = (stripes + 2) // 2
@@ -218,7 +218,7 @@
         cursor[key] = slot + 1
         order[slot] = t
 
-    groups = -(-count // GROUP)
+    groups = raw.shape[0]
 
     def tile_at(g, j):
         return order[jnp.minimum(g * GROUP + j, count - 1)]
@@ -226,7 +226,10 @@
     def key_at(g, j):
         slot = g * GROUP + j
         key = tile_patch[order[jnp.minimum(slot, count - 1)]]
-        return key if count % GROUP == 0 else jnp.where(slot < count, key, -1)
+        return key if count == groups * GROUP else jnp.where(slot < count, key, -1)
+
+    def real_key(g, j):
+        return tile_patch[order[jnp.minimum(g * GROUP + j, count - 1)]]
 
     def fetch(g, carry):
         for j in range(GROUP):
@@ -262,7 +265,7 @@
         pltpu.make_async_copy(tiles.at[pl.ds(0, GROUP)], raw.at[g], sems.at[g]).wait()
 
     def warp(g):
-        slot = g & 1
+        slot = g & (shifted.shape[0] - 1)
         ids = [tile_at(g, j) for j in range(GROUP)]
         for j in range(0, GROUP, 2):
             spreads, ends, end_mats = [], [], []
@@ -318,7 +321,7 @@
             mixers[slot, k * rows : (k + 1) * rows, :] = (mixer[k * rows : (k + 1) * rows] * scale).astype(BF16)
 
     def group_sum(g, key):
-        slot = g & 1
+        slot = g & (shifted.shape[0] - 1)
         owner = jnp.concatenate(
             [jnp.where(half_row, key_at(g, j), key_at(g, j + 1)) for j in range(0, GROUP, 2)], axis=1
         )
@@ -328,7 +331,8 @@
     def match(q):
         mains, edges = [], []
         for k in range(BASES):
-            base_k = stacked[q if deferred else 0, k * rows : (k + 1) * rows, :]
+            band_k = slice(k * rows, (k + 1) * rows)
+            base_k = total[q, band_k, :].astype(BF16) if deferred else stacked[band_k, :]
             mains.append(side_by_side(base_k))
             edges.extend(border_columns(base_k, PSF_SEGMENT))
         edge = jnp.dot(jnp.concatenate(edges, axis=1), col_edge[...], preferred_element_type=F32)
@@ -341,42 +345,61 @@
 
     def close(g, key, key_end):
         def one(k, carry):
-            if deferred:
-                stacked[k] = total[...].astype(BF16)
-            else:
-                stacked[0] = total[...].astype(BF16)
-                match(k)
-            goes_on = cursor[k] < jnp.minimum((g + 1) * GROUP, count)
-
-            @pl.when(goes_on)
-            def _():
-                total[...] = group_sum(g, k + 1)
-
-            @pl.when(jnp.logical_not(goes_on))
-            def _():
-                total[...] = jnp.zeros_like(total)
-
+            stacked[...] = total[0].astype(BF16)
+            match(k)
+            total[0] = group_sum(g, k + 1)
             return carry
 
         lax.fori_loop(key, key_end, one, 0)
+
+    def share(g):
+        def one(k, carry):
+            total[k] += group_sum(g, k)
+            return carry
+
+        lax.fori_loop(real_key(g, 0) + 1, real_key(g, GROUP - 1) + 1, one, 0)
 
     for move in moves[2:]:
         move.wait()
     total[...] = jnp.zeros_like(total)
-    arrive(0)
-    warp(0)
-
-    def step(g, key):
-        arrive(g)
-        total[...] += group_sum(g - 1, key)
-        warp(g)
-        key_end = key_at(g, 0)
-        close(g - 1, key, key_end)
-        return key_end
-
-    key = lax.fori_loop(1, groups, step, jnp.int32(0))
-    total[...] += group_sum(groups - 1, key)
-    close(groups - 1, key, patches)
+    if deferred:
+        for g in range(2):
+            arrive(g)
+        for g in range(2):
+            warp(g)
+
+        def step(i, carry):
+            g = 2 * i
+            for j in range(2):
+                arrive(g + j)
+            for j in range(2):
+                total[real_key(g - 2 + j, 0)] += group_sum(g - 2 + j, real_key(g - 2 + j, 0))
+            for j in range(2):
+                warp(g + j)
+            for j in range(2):
+                share(g - 2 + j)
+            return carry
+
+        lax.fori_loop(1, groups // 2, step, 0)
+        for g in (groups - 2, groups - 1):
+            total[real_key(g, 0)] += group_sum(g, real_key(g, 0))
+        for g in (groups - 2, groups - 1):
+            share(g)
+    else:
+        arrive(0)
+        warp(0)
+
+        def step(g, key):
+            arrive(g)
+            total[0] += group_sum(g - 1, key)
+            warp(g)
+            key_end = real_key(g, 0)
+            close(g - 1, key, key_end)
+            return key_end
+
+        key = lax.fori_loop(1, groups, step, jnp.int32(0))
+        total[0] += group_sum(groups - 1, key)
+        close(groups - 1, key, patches)
 
     batch = math.gcd(patches, PSF_BATCH)
 
@@ -431,7 +454,9 @@
     count, rows, cols = tiles.shape
     blocks = cols // LANES
     message = message_tiles(rows, cols)
+    deferred = patches <= DEFERRED
     groups = -(-count // GROUP)
+    groups += groups % 2 if deferred else 0
     hbm = pl.BlockSpec(memory_space=pltpu.HBM)
     return pl.pallas_call(
         functools.partial(stack_kernel, bits),
@@ -444,10 +469,10 @@
         out_specs=(pl.BlockSpec(memory_space=pltpu.VMEM),) * 4,
         scratch_shapes=[
             pltpu.VMEM((groups, GROUP, rows, cols), BF16),
-            pltpu.VMEM((2, GROUP * rows, cols), BF16),
-            pltpu.VMEM((2, BASES * rows, GROUP * rows), BF16),
-            pltpu.VMEM((BASES * rows, cols), F32),
-            pltpu.VMEM((patches if patches <= DEFERRED else 1, BASES * rows, cols), BF16),
+            pltpu.VMEM((4 if deferred else 2, GROUP * rows, cols), BF16),
+            pltpu.VMEM((4 if deferred else 2, BASES * rows, GROUP * rows), BF16),
+            pltpu.VMEM((patches if deferred else 1, BASES * rows, cols), F32),
+            pltpu.VMEM((8 if deferred else BASES * rows, LANES if deferred else cols), BF16),
             pltpu.VMEM(((patches * rows // 8 + 2) * blocks, 8, LANES), F32),
             pltpu.SemaphoreType.DMA((groups,)),
             pltpu.SMEM((count,), I32),

time: 38.4 us -> 37.2 us (0.969)
  Pallas kernels: 15.4 us -> 14.2 us
    pallas_call x1, Pallas kernels: 14.1 us -> 12.9 us  [local_stacks(): pl.pallas_call(functools.partial(stack_kernel, bits), out_shape=tuple((ja...]
where the time goes in v2:
time: 37.2 us; the launch traced here: 37 us
  Pallas kernels  14.2 us (38%)
  waiting for transfers between devices  11.2 us (30%)
  starting transfers between devices  10.7 us (29%)
  between operations  0.71 us (2%)
    pallas_call x1, Pallas kernels, local_stacks(): pl.pallas_call(functools.partial(stack_kernel, bits), out_shape=tuple((ja...  12.9 us
    ppermute x3, starting transfers between devices, shards(): parts.append(lax.ppermute(summed, 'patch', hop))  5.22 us
    ppermute x3, waiting for transfers between devices, shards(): parts.append(lax.ppermute(summed, 'patch', hop))  5.09 us
    ppermute x3, starting transfers between devices, shards(): crossed = lax.ppermute(crossing, 'patch', beside)  4.74 us
    ppermute x3, waiting for transfers between devices, shards(): crossed = lax.ppermute(crossing, 'patch', beside)  3.04 us
    ppermute x1, waiting for transfers between devices, shards(): first_got = lax.ppermute(first_send, 'visit', swap)  1.67 us
    ppermute x1, waiting for transfers between devices, shards(): other = lax.ppermute(mine, 'visit', swap)  1.38 us
    pallas_call x1, Pallas kernels, shards(): pl.pallas_call(smooth_kernel, out_shape=(jax.ShapeDtypeStruct((rows, cols...  1.06 us
  transfers between devices with their start and end apart: 9, of which 6 were waited for; matrix products, arithmetic and copies ran while one was open for 1% of the time, Pallas kernels for 0%

profile of v2, /device:TPU:0, one launch (start us, length us, event | category | flops | bytes accessed | tf_op | source)
XLA Modules:
  0.0 37.0 jit_solution(13529656971944119926)
XLA Ops:
  0.6 0.0 copy-start
  0.6 0.0 copy-start.1
  0.7 12.9 %stacks.1 = (bf16[2,41,8,128]{3,2,1,0:T(8,128)(2,1)S(1)}, bf16[6,41,8,128]{3,2,1,0:T(8,128)(2,1)S(1)}, f32[2,41,8,128]{3,2,1,0:T(8,128)S(1)}, f32[6,41,8,128]{3,2,1,0:T(8,128)S(1)}) custom-call(s32[56]{0:T(128)} %tile_patch_in.1, bf16[56]{0:T(256)(128)(2,1)} %raw_weights_in.1, s32[2,56]{1,0:T(2,128)} %bitcast.13, s32[3,56]{1,0:T(4,128)} %bitcast.12, ...), custom_call_target="tpu_custom_call" | custom-call | flops 7516192768 | bytes 3670016 | tf_op jit(solution)/shard_map/stacks/pallas_call | solution.py:461
  13.6 0.6 %collective-permute-start = (bf16[6,41,8,128]{3,2,1,0:T(8,128)(2,1)S(1)}, bf16[6,41,8,128]{3,2,1,0:T(8,128)(2,1)S(1)}, u32[]{:S(2)}, u32[]{:S(2)}) collective-permute-start(bf16[6,41,8,128]{3,2,1,0:T(8,128)(2,1)S(1)} %get-tuple-element.9), channel_id=1, source_target_pairs={{0,1},{1,0},{2,3},{3,2},{4,5},{5,4},{6,7},{7,6},{8,9},{9,8},{10,11... | collective-permute-start | bytes 1511432 | tf_op jit(solution)/shard_map/ppermute | solution.py:572
  14.1 0.1 collective-permute-start.1
  14.2 1.7 %collective-permute-done.1.got = bf16[2,41,8,128]{3,2,1,0:T(8,128)(2,1)S(1)} collective-permute-done((bf16[2,41,8,128]{3,2,1,0:T(8,128)(2,1)S(1)}, bf16[2,41,8,128]{3,2,1,0:T(8,128)(2,1)S(1)}, u32[]{:S(2)}, u32[]{:S(2)}) %collective-permute-start.1) | collective-permute-done | bytes 167968 | tf_op jit(solution)/shard_map/ppermute | solution.py:562
  15.9 2.6 %collective-permute-start.2 = (bf16[1,41,8,128]{3,2,1,0:T(8,128)(2,1)S(1)}, bf16[1,41,8,128]{3,2,1,0:T(8,128)(2,1)S(1)}, u32[]{:S(2)}, u32[]{:S(2)}) collective-permute-start(bf16[1,41,8,128]{3,2,1,0:T(8,128)(2,1)S(1)} %get-tuple-element.12), channel_id=1, source_target_pairs={{0,2},{2,0},{4,6},{6,4},{8,10},{10,8},{12,14},{14,12},{1,3},{3,1},... | collective-permute-start | bytes 251912 | tf_op jit(solution)/shard_map/ppermute | solution.py:577
  18.6 0.1 collective-permute-start.4
  18.6 0.0 collective-permute-done
  18.6 0.1 convert_add_fusion
  18.8 2.0 %collective-permute-start.6 = (bf16[2,41,8,128]{3,2,1,0:T(8,128)(2,1)S(1)}, bf16[2,41,8,128]{3,2,1,0:T(8,128)(2,1)S(1)}, u32[]{:S(2)}, u32[]{:S(2)}) collective-permute-start(bf16[2,41,8,128]{3,2,1,0:T(8,128)(2,1)S(1)} %slice.60), channel_id=1, source_target_pairs={{0,2},{2,0},{4,6},{6,4},{8,10},{10,8},{12,14},{14,12},{1,3},{3,1},... | collective-permute-start | bytes 503816 | tf_op jit(solution)/shard_map/ppermute | solution.py:577
  20.8 0.9 %collective-permute-done.2 = bf16[1,41,8,128]{3,2,1,0:T(8,128)(2,1)S(1)} collective-permute-done((bf16[1,41,8,128]{3,2,1,0:T(8,128)(2,1)S(1)}, bf16[1,41,8,128]{3,2,1,0:T(8,128)(2,1)S(1)}, u32[]{:S(2)}, u32[]{:S(2)}) %collective-permute-start.2) | collective-permute-done | bytes 84000 | tf_op jit(solution)/shard_map/ppermute | solution.py:577
  21.7 2.2 %collective-permute-done.4 = bf16[1,41,8,128]{3,2,1,0:T(8,128)(2,1)S(1)} collective-permute-done((bf16[1,41,8,128]{3,2,1,0:T(8,128)(2,1)S(1)}, bf16[1,41,8,128]{3,2,1,0:T(8,128)(2,1)S(1)}, u32[]{:S(2)}, u32[]{:S(2)}) %collective-permute-start.4) | collective-permute-done | bytes 84000 | tf_op jit(solution)/shard_map/ppermute | solution.py:577
  23.9 4.2 %collective-permute-start.5 = (bf16[41,8,128]{2,1,0:T(8,128)(2,1)S(1)}, bf16[41,8,128]{2,1,0:T(8,128)(2,1)S(1)}, u32[]{:S(2)}, u32[]{:S(2)}) collective-permute-start(bf16[41,8,128]{2,1,0:T(8,128)(2,1)S(1)} %fusion.2), channel_id=1, source_target_pairs={{0,12},{2,14},{4,8},{6,10},{8,4},{10,6},{12,0},{14,2},{1,13},{3,15... | collective-permute-start | bytes 251912 | tf_op jit(solution)/shard_map/ppermute | solution.py:586
  28.1 0.0 collective-permute-start.3
  28.1 0.0 collective-permute-done.6
  28.2 1.0 %collective-permute-start.7 = (bf16[41,8,128]{2,1,0:T(8,128)(2,1)S(1)}, bf16[41,8,128]{2,1,0:T(8,128)(2,1)S(1)}, u32[]{:S(2)}, u32[]{:S(2)}) collective-permute-start(bf16[41,8,128]{2,1,0:T(8,128)(2,1)S(1)} %fusion.4), channel_id=1, source_target_pairs={{0,4},{2,6},{4,0},{6,2},{8,12},{10,14},{12,8},{14,10},{1,5},{3,7},... | collective-permute-start | bytes 251912 | tf_op jit(solution)/shard_map/ppermute | solution.py:586
  29.2 1.6 %collective-permute-done.5.refs_2_ = bf16[41,8,128]{2,1,0:T(8,128)(2,1)S(1)} collective-permute-done((bf16[41,8,128]{2,1,0:T(8,128)(2,1)S(1)}, bf16[41,8,128]{2,1,0:T(8,128)(2,1)S(1)}, u32[]{:S(2)}, u32[]{:S(2)}) %collective-permute-start.5) | collective-permute-done | bytes 84000 | tf_op jit(solution)/shard_map/ppermute | solution.py:586
  30.8 3.5 %collective-permute-done.3.refs_1_ = bf16[41,8,128]{2,1,0:T(8,128)(2,1)S(1)} collective-permute-done((bf16[41,8,128]{2,1,0:T(8,128)(2,1)S(1)}, bf16[41,8,128]{2,1,0:T(8,128)(2,1)S(1)}, u32[]{:S(2)}, u32[]{:S(2)}) %collective-permute-start.3) | collective-permute-done | bytes 84000 | tf_op jit(solution)/shard_map/ppermute | solution.py:586
  34.3 0.0 collective-permute-done.7.refs_4_
  34.3 0.2 merge.1.mine
  34.5 0.1 collective-permute-start.8
  34.6 1.4 %collective-permute-done.8.other = f32[40,1024]{1,0:T(8,128)S(1)} collective-permute-done((f32[40,1024]{1,0:T(8,128)S(1)}, f32[40,1024]{1,0:T(8,128)S(1)}, u32[]{:S(2)}, u32[]{:S(2)}) %collective-permute-start.8) | collective-permute-done | bytes 163872 | tf_op jit(solution)/shard_map/ppermute | solution.py:593
  36.0 0.0 copy-done
  36.0 0.0 copy-done.1
  36.0 1.1 %smooth.1 = (f32[64,1024]{1,0:T(8,128)}, f32[64,1024]{1,0:T(8,128)}) custom-call(bf16[64,80]{1,0:T(8,128)(2,1)S(1)} %copy-done.1, bf16[256,128]{1,0:T(8,128)(2,1)S(1)} %copy-done, f32[40,1024]{1,0:T(8,128)S(1)} %merge.1.mine, f32[40,1024]{1,0:T(8,128)S(1)} %collective-permute-done.8.other), custom_call_target="tpu_custom_call" | custom-call | tf_op jit(solution)/shard_map/smooth/pallas_call | solution.py:598
  (7 shorter events, 0.2 us)
Async XLA Ops:
  0.6 35.3 %copy-start = (bf16[256,128]{1,0:T(8,128)(2,1)S(1)}, bf16[256,128]{1,0:T(8,128)(2,1)}, u32[]{:S(2)}) copy-start(bf16[256,128]{1,0:T(8,128)(2,1)} %constant.17.clone.cols_mat) | copy-start | bytes 196612
  0.6 35.3 %copy-start.1 = (bf16[64,80]{1,0:T(8,128)(2,1)S(1)}, bf16[64,80]{1,0:T(8,128)(2,1)}, u32[]{:S(2)}) copy-start(bf16[64,80]{1,0:T(8,128)(2,1)} %constant.16.clone.rows_mat) | copy-start | bytes 30724
  13.6 5.1 %collective-permute-start = (bf16[6,41,8,128]{3,2,1,0:T(8,128)(2,1)S(1)}, bf16[6,41,8,128]{3,2,1,0:T(8,128)(2,1)S(1)}, u32[]{:S(2)}, u32[]{:S(2)}) collective-permute-start(bf16[6,41,8,128]{3,2,1,0:T(8,128)(2,1)S(1)} %get-tuple-element.9), channel_id=1, source_target_pairs={{0,1},{1,0},{2,3},{3,2},{4,5},{5,4},{6,7},{7,6},{8,9},{9,8},{10,11... | collective-permute-start | bytes 1511432 | tf_op jit(solution)/shard_map/ppermute | solution.py:572
  14.1 1.7 %collective-permute-start.1 = (bf16[2,41,8,128]{3,2,1,0:T(8,128)(2,1)S(1)}, bf16[2,41,8,128]{3,2,1,0:T(8,128)(2,1)S(1)}, u32[]{:S(2)}, u32[]{:S(2)}) collective-permute-start(bf16[2,41,8,128]{3,2,1,0:T(8,128)(2,1)S(1)} %get-tuple-element.11), channel_id=1, source_target_pairs={{0,1},{1,0},{2,3},{3,2},{4,5},{5,4},{6,7},{7,6},{8,9},{9,8},{10,11... | collective-permute-start | bytes 503816 | tf_op jit(solution)/shard_map/ppermute | solution.py:562
  15.9 5.8 %collective-permute-start.2 = (bf16[1,41,8,128]{3,2,1,0:T(8,128)(2,1)S(1)}, bf16[1,41,8,128]{3,2,1,0:T(8,128)(2,1)S(1)}, u32[]{:S(2)}, u32[]{:S(2)}) collective-permute-start(bf16[1,41,8,128]{3,2,1,0:T(8,128)(2,1)S(1)} %get-tuple-element.12), channel_id=1, source_target_pairs={{0,2},{2,0},{4,6},{6,4},{8,10},{10,8},{12,14},{14,12},{1,3},{3,1},... | collective-permute-start | bytes 251912 | tf_op jit(solution)/shard_map/ppermute | solution.py:577
  18.6 5.4 %collective-permute-start.4 = (bf16[1,41,8,128]{3,2,1,0:T(8,128)(2,1)S(1)}, bf16[1,41,8,128]{3,2,1,0:T(8,128)(2,1)S(1)}, u32[]{:S(2)}, u32[]{:S(2)}) collective-permute-start(bf16[1,41,8,128]{3,2,1,0:T(8,128)(2,1)S(1)} %get-tuple-element.13), channel_id=1, source_target_pairs={{0,2},{2,0},{4,6},{6,4},{8,10},{10,8},{12,14},{14,12},{1,3},{3,1},... | collective-permute-start | bytes 251912 | tf_op jit(solution)/shard_map/ppermute | solution.py:577
  18.8 9.3 %collective-permute-start.6 = (bf16[2,41,8,128]{3,2,1,0:T(8,128)(2,1)S(1)}, bf16[2,41,8,128]{3,2,1,0:T(8,128)(2,1)S(1)}, u32[]{:S(2)}, u32[]{:S(2)}) collective-permute-start(bf16[2,41,8,128]{3,2,1,0:T(8,128)(2,1)S(1)} %slice.60), channel_id=1, source_target_pairs={{0,2},{2,0},{4,6},{6,4},{8,10},{10,8},{12,14},{14,12},{1,3},{3,1},... | collective-permute-start | bytes 503816 | tf_op jit(solution)/shard_map/ppermute | solution.py:577
  23.9 6.9 %collective-permute-start.5 = (bf16[41,8,128]{2,1,0:T(8,128)(2,1)S(1)}, bf16[41,8,128]{2,1,0:T(8,128)(2,1)S(1)}, u32[]{:S(2)}, u32[]{:S(2)}) collective-permute-start(bf16[41,8,128]{2,1,0:T(8,128)(2,1)S(1)} %fusion.2), channel_id=1, source_target_pairs={{0,12},{2,14},{4,8},{6,10},{8,4},{10,6},{12,0},{14,2},{1,13},{3,15... | collective-permute-start | bytes 251912 | tf_op jit(solution)/shard_map/ppermute | solution.py:586
  28.1 6.2 %collective-permute-start.3 = (bf16[41,8,128]{2,1,0:T(8,128)(2,1)S(1)}, bf16[41,8,128]{2,1,0:T(8,128)(2,1)S(1)}, u32[]{:S(2)}, u32[]{:S(2)}) collective-permute-start(bf16[41,8,128]{2,1,0:T(8,128)(2,1)S(1)} %get-tuple-element.15), channel_id=1, source_target_pairs={{0,8},{2,10},{4,12},{6,14},{8,0},{10,2},{12,4},{14,6},{1,9},{3,11}... | collective-permute-start | bytes 251912 | tf_op jit(solution)/shard_map/ppermute | solution.py:586
  28.2 6.1 %collective-permute-start.7 = (bf16[41,8,128]{2,1,0:T(8,128)(2,1)S(1)}, bf16[41,8,128]{2,1,0:T(8,128)(2,1)S(1)}, u32[]{:S(2)}, u32[]{:S(2)}) collective-permute-start(bf16[41,8,128]{2,1,0:T(8,128)(2,1)S(1)} %fusion.4), channel_id=1, source_target_pairs={{0,4},{2,6},{4,0},{6,2},{8,12},{10,14},{12,8},{14,10},{1,5},{3,7},... | collective-permute-start | bytes 251912 | tf_op jit(solution)/shard_map/ppermute | solution.py:586
  34.5 1.5 %collective-permute-start.8 = (f32[40,1024]{1,0:T(8,128)S(1)}, f32[40,1024]{1,0:T(8,128)S(1)}, u32[]{:S(2)}, u32[]{:S(2)}) collective-permute-start(f32[40,1024]{1,0:T(8,128)S(1)} %merge.1.mine), channel_id=1, source_target_pairs={{0,1},{1,0},{2,3},{3,2},{4,5},{5,4},{6,7},{7,6},{8,9},{9,8},{10,11... | collective-permute-start | bytes 491528 | tf_op jit(solution)/shard_map/ppermute | solution.py:593
